TPU v7x, 512 devices: a whole 4x8x8 slice. The times are simulated.
512 devices in a mesh: span: 16 (over z_hi, x), wall: 16 (over y, core), stream: 2 (over z_lo).
Axes of the slice: x: 4, y: 8, z: 8 (z_hi: 4, z_lo: 2; z = z_hi * 2 + z_lo), core: 2. Of those that a mesh axis runs over, the one named last changes fastest.
Arguments:
- fields: float32 [4, 16, 256, 2048], P(None, 'stream', 'wall', 'span'), may hold values from -67.5 to 67.5, as said below
Outputs:
- clark_model: float32 [3, 16, 256, 2048], P(None, 'stream', 'wall', 'span')
- similar_model: float32 [3, 16, 256, 2048], P(None, 'stream', 'wall', 'span')
- clark_corr: float32 [3, 256], P(None, 'wall')
- similar_corr: float32 [3, 256], P(None, 'wall')
Inputs may be any that keep to these rules, and one draw needn't show every extreme that they name: The fields are rough from cell to cell.
All inputs are finite; a program needn't handle non-finite values.
Results may differ from a plain program's by a relative error of at most 0.00024.
Values sent between devices are 32-bit elements; how exact they have to be, the bound alone decides.
A program may use at most 64 MiB of HBM per device.

v0:
```python
import math
import jax
import jax.numpy as jnp
from jax import lax
from jax.sharding import PartitionSpec as P

raw_taps = [math.exp(-((k - 8) ** 2) / 18.0) for k in range(17)]
filter_taps = [value / sum(raw_taps) for value in raw_taps]
clark_coef = 9.0
small_eps = 1e-06


def with_halo(cells, sides, width, closed):
    for axis, dim in sides:
        count = lax.axis_size(axis)
        ends = count if closed else count - 1
        head = lax.slice_in_dim(cells, 0, width, axis=dim)
        tail = lax.slice_in_dim(cells, cells.shape[dim] - width, cells.shape[dim], axis=dim)
        cells = jnp.concatenate(
            [
                lax.ppermute(tail, axis, [(i, (i + 1) % count) for i in range(ends)]),
                cells,
                lax.ppermute(head, axis, [((i + 1) % count, i) for i in range(ends)]),
            ],
            axis=dim,
        )
    return cells


def band_matrix(length):
    offset = (
        jnp.arange(length + 16, dtype=jnp.int32)[:, None]
        - jnp.arange(length, dtype=jnp.int32)[None, :]
    )
    matrix = jnp.zeros((length + 16, length), jnp.float32)
    for k in range(17):
        matrix = matrix + jnp.where(offset == k, filter_taps[k], 0.0).astype(jnp.float32)
    return matrix


def smooth(padded, direction, length):
    matrix = band_matrix(length)
    if direction == 3:
        return jnp.einsum("fswz,zk->fswk", padded, matrix, precision=lax.Precision.HIGHEST)
    if direction == 2:
        return jnp.einsum("fswz,wk->fskz", padded, matrix, precision=lax.Precision.HIGHEST)
    return jnp.einsum("fswz,sk->fkwz", padded, matrix, precision=lax.Precision.HIGHEST)


def with_products(quad):
    return jnp.concatenate([quad, quad[:3] * quad[3:4]], axis=0)


def filter_all(quad):
    stream_len, wall_len, span_len = (quad.shape[1], quad.shape[2], quad.shape[3])
    payload = with_products(quad)
    spanned = with_halo(payload, (("span", 3),), 8, True)
    extended = with_halo(spanned, (("wall", 2), ("stream", 1)), 8, False)
    kept = extended[:4]
    result = smooth(extended, 3, span_len)
    result = smooth(result, 2, wall_len)
    return (smooth(result, 1, stream_len), kept)


def clark_flux(means):
    padded = with_halo(means, (("span", 3),), 1, True)
    along_span = (padded[..., 2:] - padded[..., :-2]) * 0.5
    plane = with_halo(means, (("wall", 2), ("stream", 1)), 1, False)
    along_wall = (plane[:, 1:-1, 2:, :] - plane[:, 1:-1, :-2, :]) * 0.5
    along_stream = (plane[:, 2:, 1:-1, :] - plane[:, :-2, 1:-1, :]) * 0.5
    total = along_span[:3] * along_span[3:4] + along_wall[:3] * along_wall[3:4]
    total = total + along_stream[:3] * along_stream[3:4]
    return clark_coef * total


def shards(fields):
    first, unused_rim = filter_all(fields)
    means = first[:4]
    exact = first[4:] - means[:3] * means[3:4]
    second, mean_rim = filter_all(means)
    similar = second[4:] - second[:3] * second[3:4]
    clark = clark_flux(means)
    sums = (
        jnp.sum(exact * clark, axis=(1, 3)),
        jnp.sum(exact * similar, axis=(1, 3)),
        jnp.sum(exact * exact, axis=(1, 3)),
        jnp.sum(clark * clark, axis=(1, 3)),
        jnp.sum(similar * similar, axis=(1, 3)),
    )
    cross_c, cross_s, power_e, power_c, power_s = lax.psum(
        (sums[0], sums[1], sums[2], sums[3], sums[4]), ("span", "stream")
    )
    plane_cells = float(
        fields.shape[1] * fields.shape[3] * lax.axis_size("stream") * lax.axis_size("span")
    )
    cross_c = cross_c / plane_cells
    cross_s = cross_s / plane_cells
    power_e = power_e / plane_cells
    power_c = power_c / plane_cells
    power_s = power_s / plane_cells
    clark_corr = cross_c / jnp.sqrt((power_e + small_eps) * (power_c + small_eps))
    similar_corr = cross_s / jnp.sqrt((power_e + small_eps) * (power_s + small_eps))
    clark_model = clark / jnp.sqrt(power_c + small_eps)[:, None, :, None]
    similar_model = similar / jnp.sqrt(power_s + small_eps)[:, None, :, None]
    return (clark_model, similar_model, clark_corr, similar_corr)


def solution(mesh):
    return jax.shard_map(
        shards,
        mesh=mesh,
        in_specs=(P(None, "stream", "wall", "span"),),
        out_specs=(
            P(None, "stream", "wall", "span"),
            P(None, "stream", "wall", "span"),
            P(None, "wall"),
            P(None, "wall"),
        ),
        check_vma=False,
    )
```

profile of v0, /device:TPU:16, one launch (start us, length us, event | category | flops | bytes accessed | tf_op | source)
XLA Modules:
  0.0 371.7 jit_solution(2666519787292298506)
XLA Ops:
  3.7 13.1 %collective-permute-start.1 = (f32[7,8,16,8]{3,2,1,0:T(8,128)S(1)}, f32[7,8,16,8]{3,2,1,0:T(8,128)S(1)}, u32[]{:S(2)}, u32[]{:S(2)}) collective-permute-start(f32[7,8,16,8]{3,2,1,0:T(8,128)S(1)} %get-tuple-element.31), channel_id=1, source_target_pairs={{32,0},{64,32},{96,64},{128,96},{160,128},{192,160},{224,192},{256... | collective-permute-start | bytes 86024 | tf_op jit(solution)/shard_map/ppermute | solution.py:23
  16.9 1.9 collective-permute-start
  18.8 17.7 %collective-permute-done.1 = f32[7,8,16,8]{3,2,1,0:T(8,128)S(1)} collective-permute-done((f32[7,8,16,8]{3,2,1,0:T(8,128)S(1)}, f32[7,8,16,8]{3,2,1,0:T(8,128)S(1)}, u32[]{:S(2)}, u32[]{:S(2)}) %collective-permute-start.1) | collective-permute-done | bytes 28704 | tf_op jit(solution)/shard_map/ppermute | solution.py:23
  36.4 8.3 %collective-permute-done = f32[7,8,16,8]{3,2,1,0:T(8,128)S(1)} collective-permute-done((f32[7,8,16,8]{3,2,1,0:T(8,128)S(1)}, f32[7,8,16,8]{3,2,1,0:T(8,128)S(1)}, u32[]{:S(2)}, u32[]{:S(2)}) %collective-permute-start) | collective-permute-done | bytes 28704 | tf_op jit(solution)/shard_map/ppermute | solution.py:21
  46.3 1.9 collective-permute-start.3
  48.2 2.4 collective-permute-start.2
  50.6 3.6 collective-permute-done.3
  54.2 3.8 %collective-permute-done.2 = f32[7,8,8,144]{3,2,1,0:T(8,128)S(1)} collective-permute-done((f32[7,8,8,144]{3,2,1,0:T(8,128)S(1)}, f32[7,8,8,144]{3,2,1,0:T(8,128)S(1)}, u32[]{:S(2)}, u32[]{:S(2)}) %collective-permute-start.2) | collective-permute-done | bytes 258080 | tf_op jit(solution)/shard_map/ppermute | solution.py:21
  59.8 4.8 %collective-permute-start.4 = (f32[7,8,32,144]{3,2,1,0:T(8,128)S(1)}, f32[7,8,32,144]{3,2,1,0:T(8,128)S(1)}, u32[]{:S(2)}, u32[]{:S(2)}) collective-permute-start(f32[7,8,32,144]{3,2,1,0:T(8,128)S(1)} %pad_maximum_fusion.1), channel_id=1, source_target_pairs={{0,1},{2,3},{4,5},{6,7},{8,9},{10,11},{12,13},{14,15},{16,17},{18,... | collective-permute-start | bytes 3096584 | tf_op jit(solution)/shard_map/ppermute | solution.py:21
  64.5 36.9 %collective-permute-done.5 = f32[7,8,32,144]{3,2,1,0:T(8,128)S(1)} collective-permute-done((f32[7,8,32,144]{3,2,1,0:T(8,128)S(1)}, f32[7,8,32,144]{3,2,1,0:T(8,128)S(1)}, u32[]{:S(2)}, u32[]{:S(2)}) %collective-permute-start.5) | collective-permute-done | bytes 1032224 | tf_op jit(solution)/shard_map/ppermute | solution.py:23
  102.8 4.7 %fusion = f32[7,24,32,128]{3,2,1,0:T(8,128)S(1)} fusion(f32[7,8,32,144]{3,2,1,0:T(8,128)S(1)} %collective-permute-done.5, f32[7,8,8,144]{3,2,1,0:T(8,128)S(1)} %collective-permute-done.3, f32[7,8,16,8]{3,2,1,0:T(8,128)S(1)} %collective-permute-done.1, f32[3,8,16,128]{3,2,1,0:T(8,128)S(1)} %slice_multiply_fusion.5, f32[4,8,16,128]{3,2,1,0:T(8,128)S(1)} %copy-done, ...), kind=kOutput, calls=%fused_computation | convolution fusion | flops 1195444224 | bytes 5849088 | tf_op jit(solution)/shard_map/fswz,zk->fswk/dot_general | solution.py:44
  107.5 1.5 fusion.61
  110.5 1.9 collective-permute-start.13
  112.4 3.9 %collective-permute-start.12 = (f32[7,8,16,8]{3,1,2,0:T(8,128)S(1)}, f32[7,8,16,8]{3,1,2,0:T(8,128)S(1)}, u32[]{:S(2)}, u32[]{:S(2)}) collective-permute-start(f32[7,8,16,8]{3,1,2,0:T(8,128)S(1)} %get-tuple-element.28), channel_id=1, source_target_pairs={{0,32},{32,64},{64,96},{96,128},{128,160},{160,192},{192,224},{224... | collective-permute-start | bytes 86024 | tf_op jit(solution)/shard_map/ppermute | solution.py:21
  116.3 14.1 %collective-permute-done.13 = f32[7,8,16,8]{3,1,2,0:T(8,128)S(1)} collective-permute-done((f32[7,8,16,8]{3,1,2,0:T(8,128)S(1)}, f32[7,8,16,8]{3,1,2,0:T(8,128)S(1)}, u32[]{:S(2)}, u32[]{:S(2)}) %collective-permute-start.13) | collective-permute-done | bytes 28704 | tf_op jit(solution)/shard_map/ppermute | solution.py:23
  130.4 8.3 %collective-permute-done.12 = f32[7,8,16,8]{3,1,2,0:T(8,128)S(1)} collective-permute-done((f32[7,8,16,8]{3,1,2,0:T(8,128)S(1)}, f32[7,8,16,8]{3,1,2,0:T(8,128)S(1)}, u32[]{:S(2)}, u32[]{:S(2)}) %collective-permute-start.12) | collective-permute-done | bytes 28704 | tf_op jit(solution)/shard_map/ppermute | solution.py:21
  139.3 1.9 collective-permute-start.15
  141.2 2.4 collective-permute-start.14
  143.6 3.6 collective-permute-done.15
  147.2 3.8 %collective-permute-done.14 = f32[7,8,8,144]{3,1,2,0:T(8,128)S(1)} collective-permute-done((f32[7,8,8,144]{3,1,2,0:T(8,128)S(1)}, f32[7,8,8,144]{3,1,2,0:T(8,128)S(1)}, u32[]{:S(2)}, u32[]{:S(2)}) %collective-permute-start.14) | collective-permute-done | bytes 258080 | tf_op jit(solution)/shard_map/ppermute | solution.py:21
  152.7 4.8 %collective-permute-start.16 = (f32[7,8,32,144]{3,1,2,0:T(8,128)S(1)}, f32[7,8,32,144]{3,1,2,0:T(8,128)S(1)}, u32[]{:S(2)}, u32[]{:S(2)}) collective-permute-start(f32[7,8,32,144]{3,1,2,0:T(8,128)S(1)} %pad_maximum_fusion.2), channel_id=1, source_target_pairs={{0,1},{2,3},{4,5},{6,7},{8,9},{10,11},{12,13},{14,15},{16,17},{18,... | collective-permute-start | bytes 3096584 | tf_op jit(solution)/shard_map/ppermute | solution.py:21
  157.5 3.3 collective-permute-start.9
  160.8 2.5 collective-permute-start.8
  163.3 3.1 collective-permute-done.8
  169.2 1.9 collective-permute-start.7
  171.2 38.2 %collective-permute-done.7 = f32[4,8,16,1]{3,1,2,0:T(8,128)S(1)} collective-permute-done((f32[4,8,16,1]{3,1,2,0:T(8,128)S(1)}, f32[4,8,16,1]{3,1,2,0:T(8,128)S(1)}, u32[]{:S(2)}, u32[]{:S(2)}) %collective-permute-start.7) | collective-permute-done | bytes 2080 | tf_op jit(solution)/shard_map/ppermute | solution.py:21
  209.3 1.9 collective-permute-start.6
  211.2 8.4 %collective-permute-done.6 = f32[4,8,16,1]{3,1,2,0:T(8,128)S(1)} collective-permute-done((f32[4,8,16,1]{3,1,2,0:T(8,128)S(1)}, f32[4,8,16,1]{3,1,2,0:T(8,128)S(1)}, u32[]{:S(2)}, u32[]{:S(2)}) %collective-permute-start.6) | collective-permute-done | bytes 2080 | tf_op jit(solution)/shard_map/ppermute | solution.py:23
  220.1 2.6 pad_maximum_fusion
  222.7 5.8 %fusion.16 = f32[7,24,32,128]{3,2,1,0:T(8,128)S(1)} fusion(f32[7,24,32,144]{3,1,2,0:T(8,128)S(1)} %pad_maximum_fusion), kind=kOutput, calls=%fused_computation.17 | convolution fusion | flops 1190025216 | bytes 5849088 | tf_op jit(solution)/shard_map/fswz,zk->fswk/dot_general | solution.py:44
  228.5 1.5 fusion.59
  231.8 137.7 %all-reduce = (f32[3,16]{1,0:T(4,128)S(1)}, f32[3,16]{1,0:T(4,128)S(1)}, f32[3,16]{1,0:T(4,128)S(1)}, f32[3,16]{1,0:T(4,128)S(1)}, f32[3,16]{1,0:T(4,128)S(1)}) all-reduce(f32[3,16]{1,0:T(4,128)S(1)} %get-tuple-element.11, f32[3,16]{1,0:T(4,128)S(1)} %get-tuple-element.12, ...), channel_id=1, replica_groups=mesh['span'=16,'wall'=16,'stream'=2] {'span','stream'}, use_global_device_ids=true, to_apply=%region_1.2 | all-reduce | flops 240 | bytes 1920 | tf_op jit(solution)/shard_map/psum | solution.py:90
  (40 shorter events, 18.4 us)
Async XLA Ops:
  2.4 55.6 %copy-start = (f32[4,8,16,128]{3,2,1,0:T(8,128)S(1)}, f32[4,8,16,128]{3,2,1,0:T(8,128)}, u32[]{:S(2)}) copy-start(f32[4,8,16,128]{3,2,1,0:T(8,128)} %param.1) | copy-start | bytes 786436
  3.7 32.7 %collective-permute-start.1 = (f32[7,8,16,8]{3,2,1,0:T(8,128)S(1)}, f32[7,8,16,8]{3,2,1,0:T(8,128)S(1)}, u32[]{:S(2)}, u32[]{:S(2)}) collective-permute-start(f32[7,8,16,8]{3,2,1,0:T(8,128)S(1)} %get-tuple-element.31), channel_id=1, source_target_pairs={{32,0},{64,32},{96,64},{128,96},{160,128},{192,160},{224,192},{256... | collective-permute-start | bytes 86024 | tf_op jit(solution)/shard_map/ppermute | solution.py:23
  16.9 27.9 %collective-permute-start = (f32[7,8,16,8]{3,2,1,0:T(8,128)S(1)}, f32[7,8,16,8]{3,2,1,0:T(8,128)S(1)}, u32[]{:S(2)}, u32[]{:S(2)}) collective-permute-start(f32[7,8,16,8]{3,2,1,0:T(8,128)S(1)} %get-tuple-element.30), channel_id=1, source_target_pairs={{0,32},{32,64},{64,96},{96,128},{128,160},{160,192},{192,224},{224... | collective-permute-start | bytes 86024 | tf_op jit(solution)/shard_map/ppermute | solution.py:21
  46.3 7.9 %collective-permute-start.3 = (f32[7,8,8,144]{3,2,1,0:T(8,128)S(1)}, f32[7,8,8,144]{3,2,1,0:T(8,128)S(1)}, u32[]{:S(2)}, u32[]{:S(2)}) collective-permute-start(f32[7,8,8,144]{3,2,1,0:T(8,128)S(1)} %get-tuple-element.23), channel_id=1, source_target_pairs={{2,0},{4,2},{6,4},{8,6},{10,8},{12,10},{14,12},{16,14},{18,16},{20... | collective-permute-start | bytes 774152 | tf_op jit(solution)/shard_map/ppermute | solution.py:23
  48.2 9.8 %collective-permute-start.2 = (f32[7,8,8,144]{3,2,1,0:T(8,128)S(1)}, f32[7,8,8,144]{3,2,1,0:T(8,128)S(1)}, u32[]{:S(2)}, u32[]{:S(2)}) collective-permute-start(f32[7,8,8,144]{3,2,1,0:T(8,128)S(1)} %get-tuple-element.22), channel_id=1, source_target_pairs={{0,2},{2,4},{4,6},{6,8},{8,10},{10,12},{12,14},{14,16},{16,18},{18... | collective-permute-start | bytes 774152 | tf_op jit(solution)/shard_map/ppermute | solution.py:21
  58.5 43.0 %collective-permute-start.5 = (f32[7,8,32,144]{3,2,1,0:T(8,128)S(1)}, f32[7,8,32,144]{3,2,1,0:T(8,128)S(1)}, u32[]{:S(2)}, u32[]{:S(2)}) collective-permute-start(f32[7,8,32,144]{3,2,1,0:T(8,128)S(1)} %pad_maximum_fusion.1), channel_id=1, source_target_pairs={{1,0},{3,2},{5,4},{7,6},{9,8},{11,10},{13,12},{15,14},{17,16},{19,... | collective-permute-start | bytes 3096584 | tf_op jit(solution)/shard_map/ppermute | solution.py:23
  59.8 43.0 %collective-permute-start.4 = (f32[7,8,32,144]{3,2,1,0:T(8,128)S(1)}, f32[7,8,32,144]{3,2,1,0:T(8,128)S(1)}, u32[]{:S(2)}, u32[]{:S(2)}) collective-permute-start(f32[7,8,32,144]{3,2,1,0:T(8,128)S(1)} %pad_maximum_fusion.1), channel_id=1, source_target_pairs={{0,1},{2,3},{4,5},{6,7},{8,9},{10,11},{12,13},{14,15},{16,17},{18,... | collective-permute-start | bytes 3096584 | tf_op jit(solution)/shard_map/ppermute | solution.py:21
  110.5 20.0 %collective-permute-start.13 = (f32[7,8,16,8]{3,1,2,0:T(8,128)S(1)}, f32[7,8,16,8]{3,1,2,0:T(8,128)S(1)}, u32[]{:S(2)}, u32[]{:S(2)}) collective-permute-start(f32[7,8,16,8]{3,1,2,0:T(8,128)S(1)} %get-tuple-element.29), channel_id=1, source_target_pairs={{32,0},{64,32},{96,64},{128,96},{160,128},{192,160},{224,192},{256... | collective-permute-start | bytes 86024 | tf_op jit(solution)/shard_map/ppermute | solution.py:23
  112.4 26.4 %collective-permute-start.12 = (f32[7,8,16,8]{3,1,2,0:T(8,128)S(1)}, f32[7,8,16,8]{3,1,2,0:T(8,128)S(1)}, u32[]{:S(2)}, u32[]{:S(2)}) collective-permute-start(f32[7,8,16,8]{3,1,2,0:T(8,128)S(1)} %get-tuple-element.28), channel_id=1, source_target_pairs={{0,32},{32,64},{64,96},{96,128},{128,160},{160,192},{192,224},{224... | collective-permute-start | bytes 86024 | tf_op jit(solution)/shard_map/ppermute | solution.py:21
  139.3 7.9 %collective-permute-start.15 = (f32[7,8,8,144]{3,1,2,0:T(8,128)S(1)}, f32[7,8,8,144]{3,1,2,0:T(8,128)S(1)}, u32[]{:S(2)}, u32[]{:S(2)}) collective-permute-start(f32[7,8,8,144]{3,1,2,0:T(8,128)S(1)} %get-tuple-element.21), channel_id=1, source_target_pairs={{2,0},{4,2},{6,4},{8,6},{10,8},{12,10},{14,12},{16,14},{18,16},{20... | collective-permute-start | bytes 774152 | tf_op jit(solution)/shard_map/ppermute | solution.py:23
  141.2 9.8 %collective-permute-start.14 = (f32[7,8,8,144]{3,1,2,0:T(8,128)S(1)}, f32[7,8,8,144]{3,1,2,0:T(8,128)S(1)}, u32[]{:S(2)}, u32[]{:S(2)}) collective-permute-start(f32[7,8,8,144]{3,1,2,0:T(8,128)S(1)} %get-tuple-element.20), channel_id=1, source_target_pairs={{0,2},{2,4},{4,6},{6,8},{8,10},{10,12},{12,14},{14,16},{16,18},{18... | collective-permute-start | bytes 774152 | tf_op jit(solution)/shard_map/ppermute | solution.py:21
  151.4 68.6 %collective-permute-start.17 = (f32[7,8,32,144]{3,1,2,0:T(8,128)S(1)}, f32[7,8,32,144]{3,1,2,0:T(8,128)S(1)}, u32[]{:S(2)}, u32[]{:S(2)}) collective-permute-start(f32[7,8,32,144]{3,1,2,0:T(8,128)S(1)} %pad_maximum_fusion.2), channel_id=1, source_target_pairs={{1,0},{3,2},{5,4},{7,6},{9,8},{11,10},{13,12},{15,14},{17,16},{19,... | collective-permute-start | bytes 3096584 | tf_op jit(solution)/shard_map/ppermute | solution.py:23
  152.7 67.3 %collective-permute-start.16 = (f32[7,8,32,144]{3,1,2,0:T(8,128)S(1)}, f32[7,8,32,144]{3,1,2,0:T(8,128)S(1)}, u32[]{:S(2)}, u32[]{:S(2)}) collective-permute-start(f32[7,8,32,144]{3,1,2,0:T(8,128)S(1)} %pad_maximum_fusion.2), channel_id=1, source_target_pairs={{0,1},{2,3},{4,5},{6,7},{8,9},{10,11},{12,13},{14,15},{16,17},{18,... | collective-permute-start | bytes 3096584 | tf_op jit(solution)/shard_map/ppermute | solution.py:21
  157.5 5.8 %collective-permute-start.9 = (f32[4,8,1,128]{3,1,2,0:T(8,128)S(1)}, f32[4,8,1,128]{3,1,2,0:T(8,128)S(1)}, u32[]{:S(2)}, u32[]{:S(2)}) collective-permute-start(f32[4,8,1,128]{3,1,2,0:T(8,128)S(1)} %get-tuple-element.26), channel_id=1, source_target_pairs={{0,2},{2,4},{4,6},{6,8},{8,10},{10,12},{12,14},{14,16},{16,18},{18... | collective-permute-start | bytes 49160 | tf_op jit(solution)/shard_map/ppermute | solution.py:21
  160.8 5.6 %collective-permute-start.8 = (f32[4,8,1,128]{3,1,2,0:T(8,128)S(1)}, f32[4,8,1,128]{3,1,2,0:T(8,128)S(1)}, u32[]{:S(2)}, u32[]{:S(2)}) collective-permute-start(f32[4,8,1,128]{3,1,2,0:T(8,128)S(1)} %get-tuple-element.27), channel_id=1, source_target_pairs={{2,0},{4,2},{6,4},{8,6},{10,8},{12,10},{14,12},{16,14},{18,16},{20... | collective-permute-start | bytes 49160 | tf_op jit(solution)/shard_map/ppermute | solution.py:23
  166.5 53.2 %collective-permute-start.11 = (f32[4,1,18,128]{3,1,2,0:T(1,128)S(1)}, f32[4,1,18,128]{3,1,2,0:T(1,128)S(1)}, u32[]{:S(2)}, u32[]{:S(2)}) collective-permute-start(f32[4,1,18,128]{3,1,2,0:T(1,128)S(1)} %get-tuple-element.35), channel_id=1, source_target_pairs={{0,1},{2,3},{4,5},{6,7},{8,9},{10,11},{12,13},{14,15},{16,17},{18,... | collective-permute-start | bytes 110600 | tf_op jit(solution)/shard_map/ppermute | solution.py:21
  167.8 51.9 %collective-permute-start.10 = (f32[4,1,18,128]{3,1,2,0:T(1,128)S(1)}, f32[4,1,18,128]{3,1,2,0:T(1,128)S(1)}, u32[]{:S(2)}, u32[]{:S(2)}) collective-permute-start(f32[4,1,18,128]{3,1,2,0:T(1,128)S(1)} %get-tuple-element.34), channel_id=1, source_target_pairs={{1,0},{3,2},{5,4},{7,6},{9,8},{11,10},{13,12},{15,14},{17,16},{19,... | collective-permute-start | bytes 110600 | tf_op jit(solution)/shard_map/ppermute | solution.py:23
  169.2 40.1 %collective-permute-start.7 = (f32[4,8,16,1]{3,1,2,0:T(8,128)S(1)}, f32[4,8,16,1]{3,1,2,0:T(8,128)S(1)}, u32[]{:S(2)}, u32[]{:S(2)}) collective-permute-start(f32[4,8,16,1]{3,1,2,0:T(8,128)S(1)} %get-tuple-element.25), channel_id=1, source_target_pairs={{0,32},{32,64},{64,96},{96,128},{128,160},{160,192},{192,224},{224... | collective-permute-start | bytes 6152 | tf_op jit(solution)/shard_map/ppermute | solution.py:21
  209.3 10.3 %collective-permute-start.6 = (f32[4,8,16,1]{3,1,2,0:T(8,128)S(1)}, f32[4,8,16,1]{3,1,2,0:T(8,128)S(1)}, u32[]{:S(2)}, u32[]{:S(2)}) collective-permute-start(f32[4,8,16,1]{3,1,2,0:T(8,128)S(1)} %get-tuple-element.24), channel_id=1, source_target_pairs={{32,0},{64,32},{96,64},{128,96},{160,128},{192,160},{224,192},{256... | collective-permute-start | bytes 6152 | tf_op jit(solution)/shard_map/ppermute | solution.py:23
where the time goes:
time: 372 us
  waiting for transfers between devices  151 us (41%)
  blocking collectives  138 us (37%)
  starting transfers between devices  53.8 us (14%)
  matrix products  15.9 us (4%)
  other arithmetic  9.48 us (3%)
    psum x1, blocking collectives, shards(): lax.psum((sums[0], sums[1], sums[2], sums[3], sums[4]), ('span', 'stream'))  138 us
    ppermute x9, waiting for transfers between devices, with_halo(): lax.ppermute(head, axis, [((i + 1) % count, i) for i in range(ends)])  87.4 us
    ppermute x9, waiting for transfers between devices, with_halo(): lax.ppermute(tail, axis, [(i, (i + 1) % count) for i in range(ends)])  63.8 us
    ppermute x9, starting transfers between devices, with_halo(): lax.ppermute(head, axis, [((i + 1) % count, i) for i in range(ends)])  27.1 us
    ppermute x9, starting transfers between devices, with_halo(): lax.ppermute(tail, axis, [(i, (i + 1) % count) for i in range(ends)])  26.7 us
    dot_general x2, matrix products, smooth(): jnp.einsum('fswz,zk->fswk', padded, matrix, precision=lax.Precision.HIGHEST)  10.5 us
  transfers between devices with their start and end apart: 18, of which 13 were waited for; matrix products, arithmetic and copies ran while one was open for 0% of the time, Pallas kernels for 0%

commit v1 on v0

--- a/solution.py
+++ b/solution.py
@@ -88,7 +88,7 @@
         jnp.sum(similar * similar, axis=(1, 3)),
     )
     cross_c, cross_s, power_e, power_c, power_s = lax.psum(
-        (sums[0], sums[1], sums[2], sums[3], sums[4]), ("span", "stream")
+        lax.psum((sums[0], sums[1], sums[2], sums[3], sums[4]), "stream"), "span"
     )
     plane_cells = float(
         fields.shape[1] * fields.shape[3] * lax.axis_size("stream") * lax.axis_size("span")

time: 372 us -> 323 us (0.87)
  blocking collectives: 138 us -> 87.8 us
    psum x1 -> x2, blocking collectives: 138 us -> 87.8 us  [the longest x1 81.1 us: shards(): lax.psum(lax.psum((sums[0], sums[1], sums[2], sums[3], sums[4]), 'stream'...]
where the time goes in v1:
time: 323 us; the launch traced here: 322 us
  waiting for transfers between devices  151 us (47%)
  blocking collectives  87.8 us (27%)
  starting transfers between devices  53.8 us (17%)
  matrix products  15.9 us (5%)
  other arithmetic  9.48 us (3%)
    ppermute x9, waiting for transfers between devices, with_halo(): lax.ppermute(head, axis, [((i + 1) % count, i) for i in range(ends)])  87.4 us
    psum x1, blocking collectives, shards(): lax.psum(lax.psum((sums[0], sums[1], sums[2], sums[3], sums[4]), 'stream'...  81.1 us
    ppermute x9, waiting for transfers between devices, with_halo(): lax.ppermute(tail, axis, [(i, (i + 1) % count) for i in range(ends)])  63.8 us
    ppermute x9, starting transfers between devices, with_halo(): lax.ppermute(head, axis, [((i + 1) % count, i) for i in range(ends)])  27.1 us
    ppermute x9, starting transfers between devices, with_halo(): lax.ppermute(tail, axis, [(i, (i + 1) % count) for i in range(ends)])  26.7 us
    dot_general x2, matrix products, smooth(): jnp.einsum('fswz,zk->fswk', padded, matrix, precision=lax.Precision.HIGHEST)  10.5 us
    psum x1, blocking collectives, shards(): lax.psum((sums[0], sums[1], sums[2], sums[3], sums[4]), 'stream')  6.7 us
  transfers between devices with their start and end apart: 18, of which 13 were waited for; matrix products, arithmetic and copies ran while one was open for 0% of the time, Pallas kernels for 0%

profile of v1, /device:TPU:16, one launch (start us, length us, event | category | flops | bytes accessed | tf_op | source)
XLA Modules:
  0.0 321.9 jit_solution(14738474464237699832)
XLA Ops:
  3.7 13.1 %collective-permute-start.1 = (f32[7,8,16,8]{3,2,1,0:T(8,128)S(1)}, f32[7,8,16,8]{3,2,1,0:T(8,128)S(1)}, u32[]{:S(2)}, u32[]{:S(2)}) collective-permute-start(f32[7,8,16,8]{3,2,1,0:T(8,128)S(1)} %get-tuple-element.36), channel_id=1, source_target_pairs={{32,0},{64,32},{96,64},{128,96},{160,128},{192,160},{224,192},{256... | collective-permute-start | bytes 86024 | tf_op jit(solution)/shard_map/ppermute | solution.py:23
  16.9 1.9 collective-permute-start
  18.8 17.7 %collective-permute-done.1 = f32[7,8,16,8]{3,2,1,0:T(8,128)S(1)} collective-permute-done((f32[7,8,16,8]{3,2,1,0:T(8,128)S(1)}, f32[7,8,16,8]{3,2,1,0:T(8,128)S(1)}, u32[]{:S(2)}, u32[]{:S(2)}) %collective-permute-start.1) | collective-permute-done | bytes 28704 | tf_op jit(solution)/shard_map/ppermute | solution.py:23
  36.4 8.3 %collective-permute-done = f32[7,8,16,8]{3,2,1,0:T(8,128)S(1)} collective-permute-done((f32[7,8,16,8]{3,2,1,0:T(8,128)S(1)}, f32[7,8,16,8]{3,2,1,0:T(8,128)S(1)}, u32[]{:S(2)}, u32[]{:S(2)}) %collective-permute-start) | collective-permute-done | bytes 28704 | tf_op jit(solution)/shard_map/ppermute | solution.py:21
  46.3 1.9 collective-permute-start.3
  48.2 2.4 collective-permute-start.2
  50.6 3.6 %collective-permute-done.3 = f32[7,8,8,144]{3,2,1,0:T(8,128)S(1)} collective-permute-done((f32[7,8,8,144]{3,2,1,0:T(8,128)S(1)}, f32[7,8,8,144]{3,2,1,0:T(8,128)S(1)}, u32[]{:S(2)}, u32[]{:S(2)}) %collective-permute-start.3) | collective-permute-done | bytes 258080 | tf_op jit(solution)/shard_map/ppermute | solution.py:23
  54.2 3.8 %collective-permute-done.2 = f32[7,8,8,144]{3,2,1,0:T(8,128)S(1)} collective-permute-done((f32[7,8,8,144]{3,2,1,0:T(8,128)S(1)}, f32[7,8,8,144]{3,2,1,0:T(8,128)S(1)}, u32[]{:S(2)}, u32[]{:S(2)}) %collective-permute-start.2) | collective-permute-done | bytes 258080 | tf_op jit(solution)/shard_map/ppermute | solution.py:21
  59.8 4.8 %collective-permute-start.4 = (f32[7,8,32,144]{3,2,1,0:T(8,128)S(1)}, f32[7,8,32,144]{3,2,1,0:T(8,128)S(1)}, u32[]{:S(2)}, u32[]{:S(2)}) collective-permute-start(f32[7,8,32,144]{3,2,1,0:T(8,128)S(1)} %pad_maximum_fusion.1), channel_id=1, source_target_pairs={{0,1},{2,3},{4,5},{6,7},{8,9},{10,11},{12,13},{14,15},{16,17},{18,... | collective-permute-start | bytes 3096584 | tf_op jit(solution)/shard_map/ppermute | solution.py:21
  64.5 36.9 %collective-permute-done.5 = f32[7,8,32,144]{3,2,1,0:T(8,128)S(1)} collective-permute-done((f32[7,8,32,144]{3,2,1,0:T(8,128)S(1)}, f32[7,8,32,144]{3,2,1,0:T(8,128)S(1)}, u32[]{:S(2)}, u32[]{:S(2)}) %collective-permute-start.5) | collective-permute-done | bytes 1032224 | tf_op jit(solution)/shard_map/ppermute | solution.py:23
  102.8 4.7 %fusion = f32[7,24,32,128]{3,2,1,0:T(8,128)S(1)} fusion(f32[7,8,32,144]{3,2,1,0:T(8,128)S(1)} %collective-permute-done.5, f32[7,8,8,144]{3,2,1,0:T(8,128)S(1)} %collective-permute-done.3, f32[7,8,16,8]{3,2,1,0:T(8,128)S(1)} %collective-permute-done.1, f32[3,8,16,128]{3,2,1,0:T(8,128)S(1)} %slice_multiply_fusion.5, f32[4,8,16,128]{3,2,1,0:T(8,128)S(1)} %copy-done, ...), kind=kOutput, calls=%fused_computation | convolution fusion | flops 1195444224 | bytes 5849088 | tf_op jit(solution)/shard_map/fswz,zk->fswk/dot_general | solution.py:44
  107.5 1.5 fusion.61
  110.5 1.9 collective-permute-start.13
  112.4 3.9 %collective-permute-start.12 = (f32[7,8,16,8]{3,1,2,0:T(8,128)S(1)}, f32[7,8,16,8]{3,1,2,0:T(8,128)S(1)}, u32[]{:S(2)}, u32[]{:S(2)}) collective-permute-start(f32[7,8,16,8]{3,1,2,0:T(8,128)S(1)} %get-tuple-element.33), channel_id=1, source_target_pairs={{0,32},{32,64},{64,96},{96,128},{128,160},{160,192},{192,224},{224... | collective-permute-start | bytes 86024 | tf_op jit(solution)/shard_map/ppermute | solution.py:21
  116.3 14.1 %collective-permute-done.13 = f32[7,8,16,8]{3,1,2,0:T(8,128)S(1)} collective-permute-done((f32[7,8,16,8]{3,1,2,0:T(8,128)S(1)}, f32[7,8,16,8]{3,1,2,0:T(8,128)S(1)}, u32[]{:S(2)}, u32[]{:S(2)}) %collective-permute-start.13) | collective-permute-done | bytes 28704 | tf_op jit(solution)/shard_map/ppermute | solution.py:23
  130.4 8.3 %collective-permute-done.12 = f32[7,8,16,8]{3,1,2,0:T(8,128)S(1)} collective-permute-done((f32[7,8,16,8]{3,1,2,0:T(8,128)S(1)}, f32[7,8,16,8]{3,1,2,0:T(8,128)S(1)}, u32[]{:S(2)}, u32[]{:S(2)}) %collective-permute-start.12) | collective-permute-done | bytes 28704 | tf_op jit(solution)/shard_map/ppermute | solution.py:21
  139.3 1.9 collective-permute-start.15
  141.2 2.4 collective-permute-start.14
  143.6 3.6 %collective-permute-done.15 = f32[7,8,8,144]{3,1,2,0:T(8,128)S(1)} collective-permute-done((f32[7,8,8,144]{3,1,2,0:T(8,128)S(1)}, f32[7,8,8,144]{3,1,2,0:T(8,128)S(1)}, u32[]{:S(2)}, u32[]{:S(2)}) %collective-permute-start.15) | collective-permute-done | bytes 258080 | tf_op jit(solution)/shard_map/ppermute | solution.py:23
  147.2 3.8 %collective-permute-done.14 = f32[7,8,8,144]{3,1,2,0:T(8,128)S(1)} collective-permute-done((f32[7,8,8,144]{3,1,2,0:T(8,128)S(1)}, f32[7,8,8,144]{3,1,2,0:T(8,128)S(1)}, u32[]{:S(2)}, u32[]{:S(2)}) %collective-permute-start.14) | collective-permute-done | bytes 258080 | tf_op jit(solution)/shard_map/ppermute | solution.py:21
  152.7 4.8 %collective-permute-start.16 = (f32[7,8,32,144]{3,1,2,0:T(8,128)S(1)}, f32[7,8,32,144]{3,1,2,0:T(8,128)S(1)}, u32[]{:S(2)}, u32[]{:S(2)}) collective-permute-start(f32[7,8,32,144]{3,1,2,0:T(8,128)S(1)} %pad_maximum_fusion.2), channel_id=1, source_target_pairs={{0,1},{2,3},{4,5},{6,7},{8,9},{10,11},{12,13},{14,15},{16,17},{18,... | collective-permute-start | bytes 3096584 | tf_op jit(solution)/shard_map/ppermute | solution.py:21
  157.5 3.3 %collective-permute-start.9 = (f32[4,8,1,128]{3,1,2,0:T(8,128)S(1)}, f32[4,8,1,128]{3,1,2,0:T(8,128)S(1)}, u32[]{:S(2)}, u32[]{:S(2)}) collective-permute-start(f32[4,8,1,128]{3,1,2,0:T(8,128)S(1)} %get-tuple-element.31), channel_id=1, source_target_pairs={{0,2},{2,4},{4,6},{6,8},{8,10},{10,12},{12,14},{14,16},{16,18},{18... | collective-permute-start | bytes 49160 | tf_op jit(solution)/shard_map/ppermute | solution.py:21
  160.8 2.5 collective-permute-start.8
  163.3 3.1 collective-permute-done.8
  169.2 1.9 collective-permute-start.7
  171.2 38.2 %collective-permute-done.7 = f32[4,8,16,1]{3,1,2,0:T(8,128)S(1)} collective-permute-done((f32[4,8,16,1]{3,1,2,0:T(8,128)S(1)}, f32[4,8,16,1]{3,1,2,0:T(8,128)S(1)}, u32[]{:S(2)}, u32[]{:S(2)}) %collective-permute-start.7) | collective-permute-done | bytes 2080 | tf_op jit(solution)/shard_map/ppermute | solution.py:21
  209.3 1.9 collective-permute-start.6
  211.2 8.4 %collective-permute-done.6 = f32[4,8,16,1]{3,1,2,0:T(8,128)S(1)} collective-permute-done((f32[4,8,16,1]{3,1,2,0:T(8,128)S(1)}, f32[4,8,16,1]{3,1,2,0:T(8,128)S(1)}, u32[]{:S(2)}, u32[]{:S(2)}) %collective-permute-start.6) | collective-permute-done | bytes 2080 | tf_op jit(solution)/shard_map/ppermute | solution.py:23
  220.1 2.6 pad_maximum_fusion
  222.7 5.8 %fusion.16 = f32[7,24,32,128]{3,2,1,0:T(8,128)S(1)} fusion(f32[7,24,32,144]{3,1,2,0:T(8,128)S(1)} %pad_maximum_fusion), kind=kOutput, calls=%fused_computation.17 | convolution fusion | flops 1190025216 | bytes 5849088 | tf_op jit(solution)/shard_map/fswz,zk->fswk/dot_general | solution.py:44
  231.8 6.7 %all-reduce.1 = (f32[3,16]{1,0:T(4,128)S(1)}, f32[3,16]{1,0:T(4,128)S(1)}, f32[3,16]{1,0:T(4,128)S(1)}, f32[3,16]{1,0:T(4,128)S(1)}, f32[3,16]{1,0:T(4,128)S(1)}) all-reduce(f32[3,16]{1,0:T(4,128)S(1)} %get-tuple-element.11, f32[3,16]{1,0:T(4,128)S(1)} %get-tuple-element.12, ...), channel_id=1, replica_groups=mesh['span'=16,'wall'=16,'stream'=2] {'stream'}, use_global_device_ids=true, to_apply=%region_1.2 | all-reduce | flops 240 | bytes 1920 | tf_op jit(solution)/shard_map/psum | solution.py:91
  238.5 81.1 %all-reduce = (f32[3,16]{1,0:T(4,128)S(1)}, f32[3,16]{1,0:T(4,128)S(1)}, f32[3,16]{1,0:T(4,128)S(1)}, f32[3,16]{1,0:T(4,128)S(1)}, f32[3,16]{1,0:T(4,128)S(1)}) all-reduce(f32[3,16]{1,0:T(4,128)S(1)} %get-tuple-element.18, f32[3,16]{1,0:T(4,128)S(1)} %get-tuple-element.19, ...), channel_id=1, replica_groups=mesh['span'=16,'wall'=16,'stream'=2] {'span'}, use_global_device_ids=true, to_apply=%region_2.3 | all-reduce | flops 240 | bytes 1920 | tf_op jit(solution)/shard_map/psum | solution.py:90
  (41 shorter events, 19.9 us)
Async XLA Ops:
  2.4 55.6 %copy-start = (f32[4,8,16,128]{3,2,1,0:T(8,128)S(1)}, f32[4,8,16,128]{3,2,1,0:T(8,128)}, u32[]{:S(2)}) copy-start(f32[4,8,16,128]{3,2,1,0:T(8,128)} %param.1) | copy-start | bytes 786436
  3.7 32.7 %collective-permute-start.1 = (f32[7,8,16,8]{3,2,1,0:T(8,128)S(1)}, f32[7,8,16,8]{3,2,1,0:T(8,128)S(1)}, u32[]{:S(2)}, u32[]{:S(2)}) collective-permute-start(f32[7,8,16,8]{3,2,1,0:T(8,128)S(1)} %get-tuple-element.36), channel_id=1, source_target_pairs={{32,0},{64,32},{96,64},{128,96},{160,128},{192,160},{224,192},{256... | collective-permute-start | bytes 86024 | tf_op jit(solution)/shard_map/ppermute | solution.py:23
  16.9 27.9 %collective-permute-start = (f32[7,8,16,8]{3,2,1,0:T(8,128)S(1)}, f32[7,8,16,8]{3,2,1,0:T(8,128)S(1)}, u32[]{:S(2)}, u32[]{:S(2)}) collective-permute-start(f32[7,8,16,8]{3,2,1,0:T(8,128)S(1)} %get-tuple-element.35), channel_id=1, source_target_pairs={{0,32},{32,64},{64,96},{96,128},{128,160},{160,192},{192,224},{224... | collective-permute-start | bytes 86024 | tf_op jit(solution)/shard_map/ppermute | solution.py:21
  46.3 7.9 %collective-permute-start.3 = (f32[7,8,8,144]{3,2,1,0:T(8,128)S(1)}, f32[7,8,8,144]{3,2,1,0:T(8,128)S(1)}, u32[]{:S(2)}, u32[]{:S(2)}) collective-permute-start(f32[7,8,8,144]{3,2,1,0:T(8,128)S(1)} %get-tuple-element.28), channel_id=1, source_target_pairs={{2,0},{4,2},{6,4},{8,6},{10,8},{12,10},{14,12},{16,14},{18,16},{20... | collective-permute-start | bytes 774152 | tf_op jit(solution)/shard_map/ppermute | solution.py:23
  48.2 9.8 %collective-permute-start.2 = (f32[7,8,8,144]{3,2,1,0:T(8,128)S(1)}, f32[7,8,8,144]{3,2,1,0:T(8,128)S(1)}, u32[]{:S(2)}, u32[]{:S(2)}) collective-permute-start(f32[7,8,8,144]{3,2,1,0:T(8,128)S(1)} %get-tuple-element.27), channel_id=1, source_target_pairs={{0,2},{2,4},{4,6},{6,8},{8,10},{10,12},{12,14},{14,16},{16,18},{18... | collective-permute-start | bytes 774152 | tf_op jit(solution)/shard_map/ppermute | solution.py:21
  58.5 43.0 %collective-permute-start.5 = (f32[7,8,32,144]{3,2,1,0:T(8,128)S(1)}, f32[7,8,32,144]{3,2,1,0:T(8,128)S(1)}, u32[]{:S(2)}, u32[]{:S(2)}) collective-permute-start(f32[7,8,32,144]{3,2,1,0:T(8,128)S(1)} %pad_maximum_fusion.1), channel_id=1, source_target_pairs={{1,0},{3,2},{5,4},{7,6},{9,8},{11,10},{13,12},{15,14},{17,16},{19,... | collective-permute-start | bytes 3096584 | tf_op jit(solution)/shard_map/ppermute | solution.py:23
  59.8 43.0 %collective-permute-start.4 = (f32[7,8,32,144]{3,2,1,0:T(8,128)S(1)}, f32[7,8,32,144]{3,2,1,0:T(8,128)S(1)}, u32[]{:S(2)}, u32[]{:S(2)}) collective-permute-start(f32[7,8,32,144]{3,2,1,0:T(8,128)S(1)} %pad_maximum_fusion.1), channel_id=1, source_target_pairs={{0,1},{2,3},{4,5},{6,7},{8,9},{10,11},{12,13},{14,15},{16,17},{18,... | collective-permute-start | bytes 3096584 | tf_op jit(solution)/shard_map/ppermute | solution.py:21
  110.5 20.0 %collective-permute-start.13 = (f32[7,8,16,8]{3,1,2,0:T(8,128)S(1)}, f32[7,8,16,8]{3,1,2,0:T(8,128)S(1)}, u32[]{:S(2)}, u32[]{:S(2)}) collective-permute-start(f32[7,8,16,8]{3,1,2,0:T(8,128)S(1)} %get-tuple-element.34), channel_id=1, source_target_pairs={{32,0},{64,32},{96,64},{128,96},{160,128},{192,160},{224,192},{256... | collective-permute-start | bytes 86024 | tf_op jit(solution)/shard_map/ppermute | solution.py:23
  112.4 26.4 %collective-permute-start.12 = (f32[7,8,16,8]{3,1,2,0:T(8,128)S(1)}, f32[7,8,16,8]{3,1,2,0:T(8,128)S(1)}, u32[]{:S(2)}, u32[]{:S(2)}) collective-permute-start(f32[7,8,16,8]{3,1,2,0:T(8,128)S(1)} %get-tuple-element.33), channel_id=1, source_target_pairs={{0,32},{32,64},{64,96},{96,128},{128,160},{160,192},{192,224},{224... | collective-permute-start | bytes 86024 | tf_op jit(solution)/shard_map/ppermute | solution.py:21
  139.3 7.9 %collective-permute-start.15 = (f32[7,8,8,144]{3,1,2,0:T(8,128)S(1)}, f32[7,8,8,144]{3,1,2,0:T(8,128)S(1)}, u32[]{:S(2)}, u32[]{:S(2)}) collective-permute-start(f32[7,8,8,144]{3,1,2,0:T(8,128)S(1)} %get-tuple-element.26), channel_id=1, source_target_pairs={{2,0},{4,2},{6,4},{8,6},{10,8},{12,10},{14,12},{16,14},{18,16},{20... | collective-permute-start | bytes 774152 | tf_op jit(solution)/shard_map/ppermute | solution.py:23
  141.2 9.8 %collective-permute-start.14 = (f32[7,8,8,144]{3,1,2,0:T(8,128)S(1)}, f32[7,8,8,144]{3,1,2,0:T(8,128)S(1)}, u32[]{:S(2)}, u32[]{:S(2)}) collective-permute-start(f32[7,8,8,144]{3,1,2,0:T(8,128)S(1)} %get-tuple-element.25), channel_id=1, source_target_pairs={{0,2},{2,4},{4,6},{6,8},{8,10},{10,12},{12,14},{14,16},{16,18},{18... | collective-permute-start | bytes 774152 | tf_op jit(solution)/shard_map/ppermute | solution.py:21
  151.4 68.6 %collective-permute-start.17 = (f32[7,8,32,144]{3,1,2,0:T(8,128)S(1)}, f32[7,8,32,144]{3,1,2,0:T(8,128)S(1)}, u32[]{:S(2)}, u32[]{:S(2)}) collective-permute-start(f32[7,8,32,144]{3,1,2,0:T(8,128)S(1)} %pad_maximum_fusion.2), channel_id=1, source_target_pairs={{1,0},{3,2},{5,4},{7,6},{9,8},{11,10},{13,12},{15,14},{17,16},{19,... | collective-permute-start | bytes 3096584 | tf_op jit(solution)/shard_map/ppermute | solution.py:23
  152.7 67.3 %collective-permute-start.16 = (f32[7,8,32,144]{3,1,2,0:T(8,128)S(1)}, f32[7,8,32,144]{3,1,2,0:T(8,128)S(1)}, u32[]{:S(2)}, u32[]{:S(2)}) collective-permute-start(f32[7,8,32,144]{3,1,2,0:T(8,128)S(1)} %pad_maximum_fusion.2), channel_id=1, source_target_pairs={{0,1},{2,3},{4,5},{6,7},{8,9},{10,11},{12,13},{14,15},{16,17},{18,... | collective-permute-start | bytes 3096584 | tf_op jit(solution)/shard_map/ppermute | solution.py:21
  157.5 5.8 %collective-permute-start.9 = (f32[4,8,1,128]{3,1,2,0:T(8,128)S(1)}, f32[4,8,1,128]{3,1,2,0:T(8,128)S(1)}, u32[]{:S(2)}, u32[]{:S(2)}) collective-permute-start(f32[4,8,1,128]{3,1,2,0:T(8,128)S(1)} %get-tuple-element.31), channel_id=1, source_target_pairs={{0,2},{2,4},{4,6},{6,8},{8,10},{10,12},{12,14},{14,16},{16,18},{18... | collective-permute-start | bytes 49160 | tf_op jit(solution)/shard_map/ppermute | solution.py:21
  160.8 5.6 %collective-permute-start.8 = (f32[4,8,1,128]{3,1,2,0:T(8,128)S(1)}, f32[4,8,1,128]{3,1,2,0:T(8,128)S(1)}, u32[]{:S(2)}, u32[]{:S(2)}) collective-permute-start(f32[4,8,1,128]{3,1,2,0:T(8,128)S(1)} %get-tuple-element.32), channel_id=1, source_target_pairs={{2,0},{4,2},{6,4},{8,6},{10,8},{12,10},{14,12},{16,14},{18,16},{20... | collective-permute-start | bytes 49160 | tf_op jit(solution)/shard_map/ppermute | solution.py:23
  166.5 53.2 %collective-permute-start.11 = (f32[4,1,18,128]{3,1,2,0:T(1,128)S(1)}, f32[4,1,18,128]{3,1,2,0:T(1,128)S(1)}, u32[]{:S(2)}, u32[]{:S(2)}) collective-permute-start(f32[4,1,18,128]{3,1,2,0:T(1,128)S(1)} %get-tuple-element.40), channel_id=1, source_target_pairs={{0,1},{2,3},{4,5},{6,7},{8,9},{10,11},{12,13},{14,15},{16,17},{18,... | collective-permute-start | bytes 110600 | tf_op jit(solution)/shard_map/ppermute | solution.py:21
  167.8 51.9 %collective-permute-start.10 = (f32[4,1,18,128]{3,1,2,0:T(1,128)S(1)}, f32[4,1,18,128]{3,1,2,0:T(1,128)S(1)}, u32[]{:S(2)}, u32[]{:S(2)}) collective-permute-start(f32[4,1,18,128]{3,1,2,0:T(1,128)S(1)} %get-tuple-element.39), channel_id=1, source_target_pairs={{1,0},{3,2},{5,4},{7,6},{9,8},{11,10},{13,12},{15,14},{17,16},{19,... | collective-permute-start | bytes 110600 | tf_op jit(solution)/shard_map/ppermute | solution.py:23
  169.2 40.1 %collective-permute-start.7 = (f32[4,8,16,1]{3,1,2,0:T(8,128)S(1)}, f32[4,8,16,1]{3,1,2,0:T(8,128)S(1)}, u32[]{:S(2)}, u32[]{:S(2)}) collective-permute-start(f32[4,8,16,1]{3,1,2,0:T(8,128)S(1)} %get-tuple-element.30), channel_id=1, source_target_pairs={{0,32},{32,64},{64,96},{96,128},{128,160},{160,192},{192,224},{224... | collective-permute-start | bytes 6152 | tf_op jit(solution)/shard_map/ppermute | solution.py:21
  209.3 10.3 %collective-permute-start.6 = (f32[4,8,16,1]{3,1,2,0:T(8,128)S(1)}, f32[4,8,16,1]{3,1,2,0:T(8,128)S(1)}, u32[]{:S(2)}, u32[]{:S(2)}) collective-permute-start(f32[4,8,16,1]{3,1,2,0:T(8,128)S(1)} %get-tuple-element.29), channel_id=1, source_target_pairs={{32,0},{64,32},{96,64},{128,96},{160,128},{192,160},{224,192},{256... | collective-permute-start | bytes 6152 | tf_op jit(solution)/shard_map/ppermute | solution.py:23
